TPU v7x, 32 devices: a whole 2x2x4 slice. The times are simulated.
32 devices in a mesh: teacher: 4 (over y, x), vocab: 8 (over z, core).
Axes of the slice: x: 2, y: 2, z: 4, core: 2. Of those that a mesh axis runs over, the one named last changes fastest.
Arguments:
- teacher_hidden: bfloat16 [4, 1024, 4096], P('teacher', 'vocab'), may hold values from -180 to 180
- teacher_head: bfloat16 [4, 4096, 32000], P('teacher', None, 'vocab'), may hold values from -0.375 to 0.375
- student_hidden: bfloat16 [1024, 4096], P('teacher'), may hold values from -180 to 180
- student_head: bfloat16 [4096, 32000], P('teacher', 'vocab'), may hold values from -0.375 to 0.375
Outputs:
- loss: float32 [], replicated
- grad_hidden: float32 [1024, 4096], P('teacher', 'vocab')
- grad_weight: float32 [4096, 32000], P('teacher', 'vocab')
All inputs are finite; a program needn't handle non-finite values.
Results may differ from a plain program's by a relative error of at most 0.0027.
Values may be sent and summed in bfloat16 or wider, within the bound.
A program may use at most 192 MiB of HBM per device.

v0:
```python
import jax
import jax.numpy as jnp
from jax import lax
from jax.sharding import PartitionSpec as P

TOK = 1024


def teacher_stats(logits):
    local_top = jnp.max(logits, axis=-1)
    top = lax.pmax(local_top, "vocab")
    shifted = jnp.exp(logits - top[:, None])
    total, moment = lax.psum(
        (jnp.sum(shifted, axis=-1), jnp.sum(shifted * logits, axis=-1)), "vocab"
    )
    return (top, total, moment)


def paired_lse(stacked):
    local_top = jnp.max(stacked, axis=-1)
    top = lax.pmax(local_top, "vocab")
    total = lax.psum(jnp.sum(jnp.exp(stacked - top[..., None]), axis=-1), "vocab")
    return top + jnp.log(total)


def per_device(teacher_hidden, teacher_head, student_hidden, student_head):
    head = teacher_head[0]
    logits = jnp.dot(
        lax.all_gather(teacher_hidden[0], "vocab", axis=0, tiled=True),
        head,
        preferred_element_type=jnp.float32,
    )
    top, total, moment = teacher_stats(logits)
    lse = top + jnp.log(total)
    entropy = lse - moment / total
    confid = jnp.exp(-entropy)
    weighted = confid[:, None] * (logits - lse[:, None])
    wsum, csum = (
        lax.psum_scatter(weighted, "teacher", scatter_dimension=0, tiled=True),
        lax.psum_scatter(confid, "teacher", scatter_dimension=0, tiled=True),
    )
    raw = wsum / csum[:, None]
    full_head = lax.all_gather(student_head, "teacher", axis=0, tiled=True)
    slog = jnp.dot(student_hidden, full_head, preferred_element_type=jnp.float32)
    both_lse = paired_lse(jnp.stack([raw, slog]))
    target = raw - both_lse[0][:, None]
    slp = slog - both_lse[1][:, None]
    probs = jnp.exp(target)
    partial_kl = jnp.sum(probs * (target - slp))
    loss = lax.psum(partial_kl, ("teacher", "vocab")) / TOK
    gradl = (jnp.exp(slp) - probs).astype(jnp.bfloat16)
    grad_hidden = lax.psum_scatter(
        lax.dot_general(
            full_head, gradl, (((1,), (1,)), ((), ())), preferred_element_type=jnp.float32
        ),
        "vocab",
        scatter_dimension=0,
        tiled=True,
    ).T
    columns = lax.all_to_all(student_hidden, "teacher", split_axis=1, concat_axis=0, tiled=True)
    all_grads = lax.all_gather(gradl, "teacher", axis=0, tiled=True)
    grad_weight = lax.dot_general(
        columns, all_grads, (((0,), (0,)), ((), ())), preferred_element_type=jnp.float32
    )
    return (loss, grad_hidden, grad_weight)


def solution(mesh):
    placed = (
        P("teacher", "vocab", None),
        P("teacher", None, "vocab"),
        P("teacher", None),
        P("teacher", "vocab"),
    )
    return jax.shard_map(
        per_device,
        mesh=mesh,
        in_specs=placed,
        out_specs=(P(), P("teacher", "vocab"), P("teacher", "vocab")),
        check_vma=False,
    )
```

profile of v0, /device:TPU:0, one launch (start us, length us, event | category | flops | bytes accessed | tf_op | source)
XLA Modules:
  0.0 849.6 jit_solution(5529223192047300215)
XLA Ops:
  7.9 86.4 %all-gather.9.cloned.1.call-done = bf16[1,1024,4096]{2,1,0:T(8,128)(2,1)} async-done(((bf16[1,128,4096]{2,1,0:T(8,128)(2,1)}), bf16[1,1024,4096]{2,1,0:T(8,128)(2,1)}) %all-gather.9.cloned.1.call-update) | async-done | bytes 8388624 | tf_op jit(solution)/shard_map/all_gather | solution.py:29
  94.4 41.8 %fusion.7 = (f32[1024]{0:T(1024)S(1)}, f32[1024,4000]{0,1:T(8,128)}) fusion(bf16[1,4096,4000]{1,2,0:T(8,128)(2,1)} %param.5, bf16[1,1024,4096]{2,1,0:T(8,128)(2,1)} %all-gather.9.cloned.1.call-done), kind=kOutput, calls=%fused_computation.20 | convolution fusion | flops 33558528000 | bytes 57544704 | tf_op jit(solution)/shard_map/dot_general | solution.py:28
  136.2 14.0 %pmax.14 = f32[1024]{0:T(1024)S(1)} all-reduce(f32[1024]{0:T(1024)S(1)} %get-tuple-element.13), channel_id=1, replica_groups=mesh['teacher'=4,'vocab'=8] {'vocab'}, use_global_device_ids=true, to_apply=%region_1.0 | all-reduce | flops 1024 | bytes 8192 | tf_op jit(solution)/shard_map/pmax | solution.py:11
  150.2 7.6 multiply_reduce_fusion
  157.8 13.9 %all-reduce.1 = (f32[1024]{0:T(1024)S(1)}, f32[1024]{0:T(1024)S(1)}) all-reduce(f32[1024]{0:T(1024)S(1)} %get-tuple-element.4, f32[1024]{0:T(1024)S(1)} %get-tuple-element.3), channel_id=1, replica_groups=mesh['teacher'=4,'vocab'=8] {'vocab'}, use_global_device_ids=true, to_apply=%region_3.0 | all-reduce | flops 2048 | bytes 16384 | tf_op jit(solution)/shard_map/psum | solution.py:13
  171.7 11.5 %subtract_multiply_fusion = f32[1024,4000]{0,1:T(8,128)} fusion(f32[1024,4000]{0,1:T(8,128)} %get-tuple-element.14, f32[1024]{0:T(1024)S(1)} %get-tuple-element.10, f32[1024]{0:T(1024)S(1)} %get-tuple-element.9), kind=kLoop, calls=%fused_computation.2 | loop fusion | flops 8192000 | bytes 32776192 | tf_op jit(solution)/shard_map/mul | solution.py:37
  185.3 10.4 %all-reduce = f32[1024]{0:T(1024)S(1)} all-reduce(f32[1024]{0:T(1024)S(1)} %get-tuple-element.9), channel_id=4, replica_groups=mesh['teacher'=4,'vocab'=8] {'teacher'}, use_global_device_ids=true, to_apply=%region_7.0.clone | all-reduce | flops 1024 | bytes 8192
  195.8 136.6 %reduce-scatter.3.cloned.1.call-done = f32[256,4000]{0,1:T(8,128)} async-done(((f32[1024,4000]{0,1:T(8,128)}), f32[256,4000]{0,1:T(8,128)}) %reduce-scatter.3.cloned.1.call-update) | async-done | bytes 4096016 | tf_op jit(solution)/shard_map/reduce_scatter | solution.py:39
  332.4 4.4 fusion.5
  336.8 288.4 %all-gather.5.cloned.1.call-done = bf16[4096,4000]{0,1:T(8,128)(2,1)} async-done(((bf16[1024,4000]{0,1:T(8,128)(2,1)}), bf16[4096,4000]{0,1:T(8,128)(2,1)}) %all-gather.5.cloned.1.call-update) | async-done | bytes 32768016 | tf_op jit(solution)/shard_map/all_gather | solution.py:43
  625.1 14.1 %fusion.8 = f32[256,4000]{0,1:T(8,128)S(1)} fusion(bf16[256,4096]{1,0:T(8,128)(2,1)S(1)} %copy-done.2, bf16[4096,4000]{0,1:T(8,128)(2,1)} %all-gather.5.cloned.1.call-done), kind=kOutput, calls=%fused_computation.21 | convolution fusion | flops 8388608000 | bytes 38961152 | tf_op jit(solution)/shard_map/dot_general | solution.py:44
  639.3 2.0 copy-done.1
  641.8 16.3 %pmax.15 = f32[2,256]{1,0:T(2,128)S(1)} all-reduce(f32[2,256]{1,0:T(2,128)S(1)} %fusion.4), channel_id=1, replica_groups=mesh['teacher'=4,'vocab'=8] {'vocab'}, use_global_device_ids=true, to_apply=%region_9.0 | all-reduce | flops 512 | bytes 4096 | tf_op jit(solution)/shard_map/pmax | solution.py:21
  658.2 4.0 exponential_reduce_fusion
  662.1 13.8 %psum.30 = f32[2,256]{1,0:T(2,128)S(1)} all-reduce(f32[2,256]{1,0:T(2,128)S(1)} %exponential_reduce_fusion), channel_id=1, replica_groups=mesh['teacher'=4,'vocab'=8] {'vocab'}, use_global_device_ids=true, to_apply=%region_11.0 | all-reduce | flops 512 | bytes 4096 | tf_op jit(solution)/shard_map/psum | solution.py:22
  675.9 6.9 subtract_convert_fusion
  682.9 18.8 %convolution_bitcast_fusion.1 = f32[4096,256]{0,1:T(8,128)} fusion(bf16[256,4000]{0,1:T(8,128)(2,1)} %get-tuple-element.7, bf16[4096,4000]{0,1:T(8,128)(2,1)} %all-gather.5.cloned.1.call-done), kind=kOutput, calls=%fused_computation.11 | convolution fusion | flops 8388608000 | bytes 39010304 | tf_op jit(solution)/shard_map/dot_general | solution.py:53
  701.8 2.5 copy.9
  704.2 32.7 %all_to_all.19 = bf16[256,4,1024]{0,2,1:T(8,128)(2,1)S(1)} all-to-all(bf16[256,4,1024]{0,2,1:T(8,128)(2,1)} %bitcast.33), channel_id=1, replica_groups=mesh['teacher'=4,'vocab'=8] {'teacher'}, dimensions={1} | all-to-all | bytes 4194304 | tf_op jit(solution)/shard_map/all_to_all | solution.py:60
  736.9 2.5 copy.10
  739.4 40.0 %psum.31 = f32[]{:T(128)} all-reduce(f32[]{:T(128)} %get-tuple-element.8), channel_id=1, replica_groups=mesh['teacher'=4,'vocab'=8] {'teacher','vocab'}, use_global_device_ids=true, to_apply=%region_13.0 | all-reduce | flops 1 | bytes 8 | tf_op jit(solution)/shard_map/psum | solution.py:50
  780.0 9.0 %all-gather.7.cloned.1.call-done = bf16[1024,4000]{0,1:T(8,128)(2,1)} async-done(((bf16[256,4000]{0,1:T(8,128)(2,1)}), bf16[1024,4000]{0,1:T(8,128)(2,1)}) %all-gather.7.cloned.1.call-update) | async-done | bytes 8192016 | tf_op jit(solution)/shard_map/all_gather | solution.py:61
  789.1 15.9 %convolution_bitcast_fusion = f32[1024,4000]{0,1:T(8,128)} fusion(bf16[1024,4000]{0,1:T(8,128)(2,1)} %all-gather.7.cloned.1.call-done, bf16[1024,1024]{1,0:T(8,128)(2,1)} %bitcast.34), kind=kOutput, calls=%fused_computation.6 | convolution fusion | flops 8388608000 | bytes 26673152 | tf_op jit(solution)/shard_map/dot_general | solution.py:62
  804.9 37.0 %reduce-scatter.5.cloned.1.call-done = f32[512,256]{0,1:T(8,128)} async-done(((f32[4096,256]{0,1:T(8,128)}), f32[512,256]{0,1:T(8,128)}) %reduce-scatter.5.cloned.1.call-update) | async-done | bytes 524304 | tf_op jit(solution)/shard_map/reduce_scatter | solution.py:52
  (23 shorter events, 2.9 us)
Async XLA Ops:
  7.2 87.2 %all-gather.9.cloned.1.call-start = ((), (), s32[]{:S(2)}) async-start(), calls=%async_computation.7 | async-start | bytes 9437184 | tf_op jit(solution)/shard_map/all_gather | solution.py:29
  7.9 324.5 %reduce-scatter.3.cloned.1.call-start = ((), (), s32[]{:S(2)}) async-start(), calls=%async_computation.3 | async-start | bytes 20480000 | tf_op jit(solution)/shard_map/reduce_scatter | solution.py:39
  183.3 0.8 copy-start.3
  183.3 441.8 %copy-start.2 = (bf16[256,4096]{1,0:T(8,128)(2,1)S(1)}, bf16[256,4096]{1,0:T(8,128)(2,1)}, u32[]{:S(2)}) copy-start(bf16[256,4096]{1,0:T(8,128)(2,1)} %param.6) | copy-start | bytes 6291460
  183.3 441.8 %all-gather.5.cloned.1.call-start = ((), (), s32[]{:S(2)}) async-start(), calls=%async_computation.4 | async-start | bytes 40960000 | tf_op jit(solution)/shard_map/all_gather | solution.py:43
  184.0 605.0 %all-gather.7.cloned.1.call-start = ((), (), s32[]{:S(2)}) async-start(), calls=%async_computation.6 | async-start | bytes 10240000 | tf_op jit(solution)/shard_map/all_gather | solution.py:61
  625.1 16.1 %copy-start = (f32[1,256,4000]{1,2,0:T(8,128)S(1)}, f32[1,256,4000]{1,2,0:T(8,128)}, u32[]{:S(2)}) copy-start(f32[1,256,4000]{1,2,0:T(8,128)} %fusion.5) | copy-start | bytes 12288004
  639.3 2.0 copy-start.1
  682.9 159.0 %reduce-scatter.5.cloned.1.call-start = ((), (), s32[]{:S(2)}) async-start(), calls=%async_computation.5 | async-start | bytes 4718592 | tf_op jit(solution)/shard_map/reduce_scatter | solution.py:52
Sparse Core Ops, SparseCore 0:
  9.6 84.7 all-gather.8
  183.4 148.9 reduce-scatter.2
  334.4 290.6 all-gather.4
  683.0 106.0 all-gather.6
  791.9 49.9 reduce-scatter.4
where the time goes:
time: 850 us
  waiting for transfers between devices  559 us (66%)
  blocking collectives  141 us (17%)
  matrix products  90.6 us (11%)
  other arithmetic  34.9 us (4%)
  between operations  16.3 us (2%)
    all_gather x1, waiting for transfers between devices, per_device(): full_head = lax.all_gather(student_head, 'teacher', axis=0, tiled=True)  288 us
    reduce_scatter x1, waiting for transfers between devices, per_device(): lax.psum_scatter(weighted, 'teacher', scatter_dimension=0, tiled=True)  137 us
    all_gather x1, waiting for transfers between devices, per_device(): lax.all_gather(teacher_hidden[0], 'vocab', axis=0, tiled=True)  86.4 us
    dot_general x1, matrix products, per_device(): jnp.dot(lax.all_gather(teacher_hidden[0], 'vocab', axis=0, tiled=True), h...  41.8 us
    psum x1, blocking collectives, per_device(): loss = lax.psum(partial_kl, ('teacher', 'vocab')) / TOK  40 us
    reduce_scatter x1, waiting for transfers between devices, per_device(): lax.psum_scatter(lax.dot_general(full_head, gradl, (((1,), (1,)), ((), ()...  37 us
    all_to_all x1, blocking collectives, per_device(): lax.all_to_all(student_hidden, 'teacher', split_axis=1, concat_axis=0, ti...  32.7 us
    dot_general x1, matrix products, per_device(): lax.dot_general(full_head, gradl, (((1,), (1,)), ((), ())), preferred_ele...  18.8 us
  transfers between devices with their start and end apart: 5, of which 5 were waited for; matrix products, arithmetic and copies ran while one was open for 5% of the time, Pallas kernels for 0%

commit v1 on v0

--- a/solution.py
+++ b/solution.py
@@ -4,6 +4,12 @@
 from jax.sharding import PartitionSpec as P
 
 TOK = 1024
+
+
+def joined_along(blocks, dim):
+    blocks = jnp.moveaxis(blocks, 0, dim)
+    shape = blocks.shape
+    return blocks.reshape(*shape[:dim], shape[dim] * shape[dim + 1], *shape[dim + 2 :])
 
 
 def teacher_stats(logits):
@@ -40,7 +46,19 @@
         lax.psum_scatter(confid, "teacher", scatter_dimension=0, tiled=True),
     )
     raw = wsum / csum[:, None]
-    full_head = lax.all_gather(student_head, "teacher", axis=0, tiled=True)
+    devices = lax.axis_size("teacher")
+    pairs = [(i, (i + 1) % devices) for i in range(devices)]
+    back = [(b, a) for a, b in pairs]
+    lower, upper = ([], [])
+    for lap in range(devices - 1):
+        if lap % 2 == 0:
+            lower.append(lax.ppermute(lower[-1] if lower else student_head, "teacher", pairs))
+        else:
+            upper.append(lax.ppermute(upper[-1] if upper else student_head, "teacher", back))
+    blocks = jnp.stack([*lower[::-1], student_head, *upper])
+    shift = lax.axis_index("teacher") - len(lower)
+    blocks = blocks[(jnp.arange(devices) - shift) % devices]
+    full_head = joined_along(blocks, 0)
     slog = jnp.dot(student_hidden, full_head, preferred_element_type=jnp.float32)
     both_lse = paired_lse(jnp.stack([raw, slog]))
     target = raw - both_lse[0][:, None]

time: 850 us -> 1230 us (1.45)
  blocking collectives: 141 us -> 473 us
  local copies, waits for them, and re-layouts: 7.62 us -> 126 us
  waiting for transfers between devices: 559 us -> 455 us
  other arithmetic: 34.9 us -> 57 us
    unnamed x1, blocking collectives: 10.4 us -> 351 us
    ppermute x0 -> x3, waiting for transfers between devices: none -> 309 us  [the longest x2 309 us: per_device(): lax.ppermute(lower[-1] if lower else student_head, 'teacher', pairs)]
    all_gather x1 -> x0, waiting for transfers between devices: 288 us -> none  [per_device(): full_head = lax.all_gather(student_head, 'teacher', axis=0, tiled=True)]
    reduce_scatter x1, waiting for transfers between devices: 137 us -> 0.01 us  [per_device(): lax.psum_scatter(weighted, 'teacher', scatter_dimension=0, tiled=True)]
    unnamed x11 -> x30, local copies, waits for them, and re-layouts: 5.11 us -> 72.1 us
    gather x0 -> x6, local copies, waits for them, and re-layouts: none -> 51 us  [per_device(): blocks = blocks[(jnp.arange(devices) - shift) % devices]]
    all_gather x1, waiting for transfers between devices: 9.04 us -> 57.9 us  [per_device(): all_grads = lax.all_gather(gradl, 'teacher', axis=0, tiled=True)]
    reduce_scatter x1, waiting for transfers between devices: 37 us -> 0.02 us  [per_device(): lax.psum_scatter(lax.dot_general(full_head, gradl, (((1,), (1,)), ((), ()...]
  transfers between devices with their start and end apart: 5 -> 7, of which waited for: 5 -> 3; matrix products, arithmetic and copies ran while one was open for 5% -> 14% of each run, Pallas kernels for 0% -> 0%
where the time goes in v1:
time: 1230 us; the launch traced here: 1220 us
  blocking collectives  473 us (38%)
  waiting for transfers between devices  455 us (37%)
  local copies, waits for them, and re-layouts  126 us (10%)
  matrix products  93.1 us (8%)
  other arithmetic  57 us (5%)
  between operations  16.3 us (1%)
    unnamed x1, blocking collectives  351 us
    ppermute x2, waiting for transfers between devices, per_device(): lax.ppermute(lower[-1] if lower else student_head, 'teacher', pairs)  309 us
    all_gather x1, waiting for transfers between devices, per_device(): lax.all_gather(teacher_hidden[0], 'vocab', axis=0, tiled=True)  86.4 us
    unnamed x30, local copies, waits for them, and re-layouts  72.1 us
    all_gather x1, waiting for transfers between devices, per_device(): all_grads = lax.all_gather(gradl, 'teacher', axis=0, tiled=True)  57.9 us
    gather x6, local copies, waits for them, and re-layouts, per_device(): blocks = blocks[(jnp.arange(devices) - shift) % devices]  51 us
    dot_general x1, matrix products, per_device(): jnp.dot(lax.all_gather(teacher_hidden[0], 'vocab', axis=0, tiled=True), h...  41.8 us
    psum x1, blocking collectives, per_device(): loss = lax.psum(partial_kl, ('teacher', 'vocab')) / TOK  37.6 us
  transfers between devices with their start and end apart: 7, of which 3 were waited for; matrix products, arithmetic and copies ran while one was open for 14% of the time, Pallas kernels for 0%

profile of v1, /device:TPU:0, one launch (start us, length us, event | category | flops | bytes accessed | tf_op | source)
XLA Modules:
  0.0 1223.9 jit_solution(12021307973292721627)
XLA Ops:
  7.9 86.4 %all-gather.6.cloned.1.call-done = bf16[1,1024,4096]{2,1,0:T(8,128)(2,1)} async-done(((bf16[1,128,4096]{2,1,0:T(8,128)(2,1)}), bf16[1,1024,4096]{2,1,0:T(8,128)(2,1)}) %all-gather.6.cloned.1.call-update) | async-done | bytes 8388624 | tf_op jit(solution)/shard_map/all_gather | solution.py:35
  94.4 41.8 %fusion.10 = (f32[1024]{0:T(1024)S(1)}, f32[1024,4000]{0,1:T(8,128)}) fusion(bf16[1,4096,4000]{1,2,0:T(8,128)(2,1)} %param.5, bf16[1,1024,4096]{2,1,0:T(8,128)(2,1)} %all-gather.6.cloned.1.call-done), kind=kOutput, calls=%fused_computation.40 | convolution fusion | flops 33558528000 | bytes 57544704 | tf_op jit(solution)/shard_map/dot_general | solution.py:34
  136.2 14.0 %pmax.14 = f32[1024]{0:T(1024)S(1)} all-reduce(f32[1024]{0:T(1024)S(1)} %get-tuple-element.29), channel_id=1, replica_groups=mesh['teacher'=4,'vocab'=8] {'vocab'}, use_global_device_ids=true, to_apply=%region_1.0 | all-reduce | flops 1024 | bytes 8192 | tf_op jit(solution)/shard_map/pmax | solution.py:17
  150.2 7.6 multiply_reduce_fusion
  157.8 13.9 %all-reduce.1 = (f32[1024]{0:T(1024)S(1)}, f32[1024]{0:T(1024)S(1)}) all-reduce(f32[1024]{0:T(1024)S(1)} %get-tuple-element.16, f32[1024]{0:T(1024)S(1)} %get-tuple-element.15), channel_id=1, replica_groups=mesh['teacher'=4,'vocab'=8] {'vocab'}, use_global_device_ids=true, to_apply=%region_3.0 | all-reduce | flops 2048 | bytes 16384 | tf_op jit(solution)/shard_map/psum | solution.py:19
  171.7 11.5 subtract_multiply_fusion
  186.3 309.1 %collective-permute-done = bf16[1024,4000]{0,1:T(8,128)(2,1)} collective-permute-done((bf16[1024,4000]{0,1:T(8,128)(2,1)}, bf16[1024,4000]{0,1:T(8,128)(2,1)}, u32[]{:S(2)}, u32[]{:S(2)}) %collective-permute-start) | collective-permute-done | bytes 8192032 | tf_op jit(solution)/shard_map/ppermute | solution.py:55
  497.5 351.2 %all-reduce = f32[1024]{0:T(1024)S(1)} all-reduce(f32[1024]{0:T(1024)S(1)} %get-tuple-element.25), channel_id=4, replica_groups=mesh['teacher'=4,'vocab'=8] {'teacher'}, use_global_device_ids=true, to_apply=%region_7.0.clone | all-reduce | flops 1024 | bytes 8192
  853.4 23.1 %pad_maximum_fusion = bf16[4,1024,4000]{1,2,0:T(8,128)(2,1)} fusion(bf16[1,1024,4000]{1,2,0:T(8,128)(2,1)} %bitcast.6, bf16[1,1024,4000]{1,2,0:T(8,128)(2,1)} %bitcast.47, bf16[1,1024,4000]{1,2,0:T(8,128)(2,1)} %bitcast.4, bf16[1,1024,4000]{1,2,0:T(8,128)(2,1)} %bitcast.3), kind=kLoop, calls=%fused_computation.5 | loop fusion | flops 49152000 | bytes 65536000 | tf_op jit(solution)/shard_map/stack | solution.py:58
  876.4 20.1 %fusion.8 = (bf16[4,1024,896]{1,2,0:T(8,128)(2,1)}, bf16[4,1024,896]{1,2,0:T(8,128)(2,1)}, bf16[4,1024,896]{1,2,0:T(8,128)(2,1)}, bf16[4,1024,896]{1,2,0:T(8,128)(2,1)}) fusion(bf16[4,1024,4000]{1,2,0:T(8,128)(2,1)} %pad_maximum_fusion), kind=kLoop, calls=%fused_computation.38 | loop fusion | bytes 58720256 | tf_op jit(solution)/shard_map/gather | solution.py:60
  896.5 7.1 gather_fusion.3
  903.6 7.1 gather_fusion.2
  917.8 7.1 gather_fusion
  924.8 7.1 constant_dynamic-update-slice_fusion.4
  935.9 7.1 constant_dynamic-update-slice_fusion.2
  948.9 39.8 %copy.14 = bf16[4,1024,4000]{2,1,0:T(8,128)(2,1)} copy(bf16[4,1024,4000]{1,2,0:T(8,128)(2,1)} %constant_dynamic-update-slice_fusion) | data formatting | bytes 65536000
  988.8 17.6 %fusion.11 = f32[4000,256]{1,0:T(8,128)} fusion(bf16[4096,4000]{1,0:T(8,128)(2,1)} %bitcast.44, bf16[256,4096]{1,0:T(8,128)(2,1)S(1)} %copy-done.5), kind=kOutput, calls=%fused_computation.41 | convolution fusion | flops 8388608000 | bytes 38961152 | tf_op jit(solution)/shard_map/dot_general | solution.py:62
  1011.6 13.6 %pmax.15 = f32[2,256]{1,0:T(2,128)S(1)} all-reduce(f32[2,256]{1,0:T(2,128)S(1)} %fusion.4), channel_id=1, replica_groups=mesh['teacher'=4,'vocab'=8] {'vocab'}, use_global_device_ids=true, to_apply=%region_9.10 | all-reduce | flops 512 | bytes 4096 | tf_op jit(solution)/shard_map/pmax | solution.py:27
  1029.2 13.9 %psum.30 = f32[2,256]{1,0:T(2,128)S(1)} all-reduce(f32[2,256]{1,0:T(2,128)S(1)} %exponential_reduce_fusion), channel_id=1, replica_groups=mesh['teacher'=4,'vocab'=8] {'vocab'}, use_global_device_ids=true, to_apply=%region_11.12 | all-reduce | flops 512 | bytes 4096 | tf_op jit(solution)/shard_map/psum | solution.py:28
  1048.6 17.8 %fusion.12 = f32[4096,256]{1,0:T(8,128)} fusion(bf16[4096,4000]{1,0:T(8,128)(2,1)} %bitcast.45, bf16[256,4000]{0,1:T(8,128)(2,1)S(1)} %get-tuple-element.23), kind=kOutput, calls=%fused_computation.42 | convolution fusion | flops 8388608000 | bytes 39010304 | tf_op jit(solution)/shard_map/dot_general | solution.py:71
  1070.6 29.0 %all_to_all.19 = bf16[256,4,1024]{0,2,1:T(8,128)(2,1)S(1)} all-to-all(bf16[256,4,1024]{0,2,1:T(8,128)(2,1)} %bitcast.51), channel_id=1, replica_groups=mesh['teacher'=4,'vocab'=8] {'teacher'}, dimensions={1} | all-to-all | bytes 4194304 | tf_op jit(solution)/shard_map/all_to_all | solution.py:78
  1102.1 37.6 %psum.31 = f32[]{:T(128)} all-reduce(f32[]{:T(128)} %get-tuple-element.24), channel_id=1, replica_groups=mesh['teacher'=4,'vocab'=8] {'teacher','vocab'}, use_global_device_ids=true, to_apply=%region_13.14 | all-reduce | flops 1 | bytes 8 | tf_op jit(solution)/shard_map/psum | solution.py:68
  1142.5 57.9 %all-gather.4.cloned.1.call-done = bf16[1024,4000]{0,1:T(8,128)(2,1)} async-done(((bf16[256,4000]{0,1:T(8,128)(2,1)}), bf16[1024,4000]{0,1:T(8,128)(2,1)}) %all-gather.4.cloned.1.call-update) | async-done | bytes 8192016 | tf_op jit(solution)/shard_map/all_gather | solution.py:79
  1200.4 15.9 %convolution_bitcast_fusion = f32[1024,4000]{0,1:T(8,128)} fusion(bf16[1024,4000]{0,1:T(8,128)(2,1)} %all-gather.4.cloned.1.call-done, bf16[1024,1024]{1,0:T(8,128)(2,1)} %bitcast.52), kind=kOutput, calls=%fused_computation.12 | convolution fusion | flops 8388608000 | bytes 26673152 | tf_op jit(solution)/shard_map/dot_general | solution.py:80
  (56 shorter events, 50.2 us)
Async XLA Ops:
  7.2 87.2 %all-gather.6.cloned.1.call-start = ((), (), s32[]{:S(2)}) async-start(), calls=%async_computation.6 | async-start | bytes 9437184 | tf_op jit(solution)/shard_map/all_gather | solution.py:35
  7.9 998.6 %reduce-scatter.3.cloned.1.call-start = ((), (), s32[]{:S(2)}) async-start(), calls=%async_computation.3 | async-start | bytes 20480000 | tf_op jit(solution)/shard_map/reduce_scatter | solution.py:45
  183.2 313.0 %copy-start.7 = (u32[32]{0:T(128)S(1)}, u32[32]{0:T(128)}, u32[]{:S(2)}) copy-start(u32[32]{0:T(128)} %constant.36) | copy-start | bytes 388
  183.3 957.2 %reduce-scatter.5.cloned.1.call-start = ((), (), s32[]{:S(2)}) async-start(), calls=%async_computation.4 | async-start | bytes 4718592 | tf_op jit(solution)/shard_map/reduce_scatter | solution.py:70
  183.3 312.1 %collective-permute-start = (bf16[1024,4000]{0,1:T(8,128)(2,1)}, bf16[1024,4000]{0,1:T(8,128)(2,1)}, u32[]{:S(2)}, u32[]{:S(2)}) collective-permute-start(bf16[1024,4000]{0,1:T(8,128)(2,1)} %param.7), channel_id=1, source_target_pairs={{0,8},{8,16},{16,24},{24,0},{1,9},{9,17},{17,25},{25,1},{2,10},{10... | collective-permute-start | bytes 24576008 | tf_op jit(solution)/shard_map/ppermute | solution.py:55
  185.1 663.7 %collective-permute-start.2 = (bf16[1024,4000]{0,1:T(8,128)(2,1)}, bf16[1024,4000]{0,1:T(8,128)(2,1)}, u32[]{:S(2)}, u32[]{:S(2)}) collective-permute-start(bf16[1024,4000]{0,1:T(8,128)(2,1)} %param.7), channel_id=1, source_target_pairs={{8,0},{16,8},{24,16},{0,24},{9,1},{17,9},{25,17},{1,25},{10,2},{18... | collective-permute-start | bytes 24576008 | tf_op jit(solution)/shard_map/ppermute | solution.py:57
  495.4 353.3 %collective-permute-start.1 = (bf16[1024,4000]{0,1:T(8,128)(2,1)}, bf16[1024,4000]{0,1:T(8,128)(2,1)}, u32[]{:S(2)}, u32[]{:S(2)}) collective-permute-start(bf16[1024,4000]{0,1:T(8,128)(2,1)} %collective-permute-done), channel_id=1, source_target_pairs={{0,8},{8,16},{16,24},{24,0},{1,9},{9,17},{17,25},{25,1},{2,10},{10... | collective-permute-start | bytes 24576008 | tf_op jit(solution)/shard_map/ppermute | solution.py:55
  924.8 7.1 copy-start.2
  932.0 11.0 slice-start
  935.9 7.1 slice-start.1
  943.0 3.9 copy-start.3
  948.9 39.9 %copy-start.5 = (bf16[256,4096]{1,0:T(8,128)(2,1)S(1)}, bf16[256,4096]{1,0:T(8,128)(2,1)}, u32[]{:S(2)}) copy-start(bf16[256,4096]{1,0:T(8,128)(2,1)} %param.6) | copy-start | bytes 6291460
  1006.5 4.6 copy-start.1
  1009.1 2.0 copy-start
  1048.6 17.8 %copy-start.4 = (bf16[256,4000]{0,1:T(8,128)(2,1)}, bf16[256,4000]{0,1:T(8,128)(2,1)S(1)}, u32[]{:S(2)}) copy-start(bf16[256,4000]{0,1:T(8,128)(2,1)S(1)} %get-tuple-element.23) | copy-start | bytes 6144004
  1066.5 1.6 copy-start.6
  1066.5 133.9 %all-gather.4.cloned.1.call-start = ((), (), s32[]{:S(2)}) async-start(), calls=%async_computation.5 | async-start | bytes 10240000 | tf_op jit(solution)/shard_map/all_gather | solution.py:79
Sparse Core Ops, SparseCore 0:
  9.6 84.7 all-gather.5
  183.4 281.6 reduce-scatter.2
  1066.6 47.2 reduce-scatter.4
  1115.7 84.6 all-gather.3
